TPU v7x, 256 devices: a whole 4x4x8 slice. The times are simulated.
256 devices in a mesh: req: 16 (over z_hi, x), mp: 16 (over z_lo, y, core).
Axes of the slice: x: 4, y: 4, z: 8 (z_hi: 4, z_lo: 2; z = z_hi * 2 + z_lo), core: 2. Of those that a mesh axis runs over, the one named last changes fastest.
Arguments:
- queries: bfloat16 [2048, 4096], P('req', 'mp'), may hold values from -6 to 6
- suffix_kv: bfloat16 [2, 2048, 4096], P(None, 'req', 'mp'), may hold values from -6 to 6
- prefix_kv: bfloat16 [2, 8192, 4096], P(None, 'req', 'mp'), may hold values from -6 to 6
- resid: bfloat16 [2048, 4096], P('req', 'mp'), may hold values from -6 to 6
- ln_gain: float32 [4096], replicated, may hold values from 0.1 to 1.9
- out_weight: bfloat16 [4096, 4096], P('mp'), may hold values from -0.125 to 0.125
- up_weight: bfloat16 [4096, 8192], P(None, 'mp'), may hold values from -0.09375 to 0.09375
- down_weight: bfloat16 [8192, 4096], P('mp'), may hold values from -0.09375 to 0.09375
- lengths: int32 [16], replicated, may hold values from 1 to 128, 1024 in all
- req_group: int32 [16], replicated, may hold values from 0 to 3, as said below
- prefix_owner: int32 [16], replicated, may hold values from 0 to 15, as said below
Outputs:
- attended: bfloat16 [2048, 4096], P('req', 'mp')
- layer_out: bfloat16 [2048, 4096], P('req', 'mp')
Inputs may be any that keep to these rules, and one draw needn't show every extreme that they name: `req_group`: each of the 4 groups holds exactly 4 requests. `prefix_owner`: a permutation: every logical block is held by exactly one stored block.
All inputs are finite; a program needn't handle non-finite values.
Results may differ from a plain program's by a relative error of at most 0.029.
Values may be sent and summed in bfloat16 or wider, within the bound.
A program may use at most 128 MiB of HBM per device.

v0:
```python
import jax
import jax.numpy as jnp
from jax import lax
from jax.sharding import PartitionSpec as P

H = 32
DH = 128
KB = 512
S_MAX = 128
P_SIZE = 2048
very_negative = -1e30


def block_partial(query_rows, key_rows, value_rows, query_pos, key_pos, allowed, slopes, shared):
    if shared:
        score_form = "rqhd,khd->rqhk"
        value_form = "rqhk,khd->rqhd"
    else:
        score_form = "rqhd,rkhd->rqhk"
        value_form = "rqhk,rkhd->rqhd"
    scores = jnp.einsum(
        score_form, query_rows, key_rows, preferred_element_type=jnp.float32
    ) * float(DH) ** (-0.5)
    distance = (query_pos[:, None, None] - key_pos[None, None, :]).astype(jnp.float32)
    scores = scores - slopes[None, :, None] * distance
    masked = jnp.where(allowed, scores, very_negative)
    maxima = jnp.max(masked, axis=-1)
    weights = jnp.where(allowed, jnp.exp(masked - maxima[..., None]), 0.0)
    totals = jnp.sum(weights, axis=-1)
    rounded = weights.astype(jnp.bfloat16)
    weighted = jnp.einsum(value_form, rounded, value_rows, preferred_element_type=jnp.float32)
    return (weighted, maxima, totals)


def combine(first_part, second_part):
    peak_max = jnp.maximum(first_part[1], second_part[1])
    scale_first = jnp.exp(first_part[1] - peak_max)
    scale_second = jnp.exp(second_part[1] - peak_max)
    weighted = first_part[0] * scale_first[..., None] + second_part[0] * scale_second[..., None]
    return (weighted, peak_max, first_part[2] * scale_first + second_part[2] * scale_second)


def shards(
    queries,
    suffix_kv,
    prefix_kv,
    resid,
    ln_gain,
    out_weight,
    up_weight,
    down_weight,
    lengths,
    req_group,
    prefix_owner,
):
    row_count = queries.shape[0]
    local_req = row_count // S_MAX
    columns = queries.shape[1]
    head_count = columns // DH
    per_group = P_SIZE // KB
    first_req = lax.axis_index("req") * local_req
    col_start = lax.axis_index("mp") * columns
    my_len = lax.dynamic_slice_in_dim(lengths, first_req, local_req)
    my_group = lax.dynamic_slice_in_dim(req_group, first_req, local_req)
    head_ids = (lax.axis_index("mp") * head_count + jnp.arange(head_count)).astype(jnp.float32)
    slopes = jnp.power(2.0, -8.0 * (head_ids + 1.0) / H)
    my_query = queries.reshape(local_req, S_MAX, head_count, DH)
    suffix_local = suffix_kv.reshape(2, local_req, S_MAX, head_count, DH)
    offsets = jnp.arange(S_MAX)
    query_pos = P_SIZE + offsets
    allowed = (offsets[None, None, :] <= offsets[None, :, None]) & (
        offsets[None, None, :] < my_len[:, None, None]
    )
    own_part = block_partial(
        my_query,
        suffix_local[0],
        suffix_local[1],
        query_pos,
        query_pos,
        allowed[:, :, None, :],
        slopes,
        False,
    )
    key_offsets = jnp.arange(KB)
    shard_piece = lax.all_gather(prefix_kv, "req", axis=1, tiled=True)
    block_total = shard_piece.shape[1] // KB
    blocks_here = shard_piece.reshape(2, block_total, KB, head_count, DH)

    def fold_step(block_index, inner_state):
        logical = prefix_owner[block_index]
        same_group = my_group == logical // per_group
        base_pos = logical % per_group * KB

        def attend_block(state_in):
            fresh = block_partial(
                my_query,
                blocks_here[0, block_index],
                blocks_here[1, block_index],
                query_pos,
                base_pos + key_offsets,
                same_group[:, None, None, None],
                slopes,
                True,
            )
            return combine(state_in, fresh)

        return lax.cond(jnp.any(same_group), attend_block, lambda state_in: state_in, inner_state)

    result = lax.fori_loop(0, block_total, fold_step, own_part)
    outcome = result[0] / result[2][..., None]
    live_mask = offsets[None, :] < my_len[:, None]
    attended = (
        jnp.where(live_mask[:, :, None, None], outcome, 0.0)
        .astype(jnp.bfloat16)
        .reshape(row_count, columns)
    )
    head_term = jnp.dot(attended, out_weight, preferred_element_type=jnp.float32)
    own_columns = lax.dynamic_slice_in_dim(head_term, col_start, columns, 1) + resid.astype(
        jnp.float32
    )
    head_term = lax.dynamic_update_slice_in_dim(head_term, own_columns, col_start, 1)
    mixed_rows = lax.psum(head_term.astype(jnp.bfloat16), "mp").astype(jnp.float32)
    row_mean = jnp.mean(mixed_rows, axis=1, keepdims=True)
    centered = mixed_rows - row_mean
    variance = jnp.mean(centered * centered, axis=1, keepdims=True)
    normed = (centered * lax.rsqrt(variance + 1e-05) * ln_gain).astype(jnp.bfloat16)
    hidden = jax.nn.gelu(
        jnp.dot(normed, up_weight, preferred_element_type=jnp.float32), approximate=False
    ).astype(jnp.bfloat16)
    projected = jnp.dot(hidden, down_weight, preferred_element_type=jnp.float32)
    update = lax.psum_scatter(
        projected.astype(jnp.bfloat16), "mp", scatter_dimension=1, tiled=True
    ).astype(jnp.float32)
    mixed_own = lax.dynamic_slice_in_dim(mixed_rows, col_start, columns, 1)
    layer_out = jnp.where(live_mask.reshape(row_count)[:, None], mixed_own + update, 0.0).astype(
        jnp.bfloat16
    )
    return (attended, layer_out)


def solution(mesh):
    placed = (
        P("req", "mp"),
        P(None, "req", "mp"),
        P(None, "req", "mp"),
        P("req", "mp"),
        P(),
        P("mp", None),
        P(None, "mp"),
        P("mp", None),
        P(),
        P(),
        P(),
    )
    return jax.shard_map(
        shards,
        mesh=mesh,
        in_specs=placed,
        out_specs=(P("req", "mp"), P("req", "mp")),
        check_vma=False,
    )
```

profile of v0, /device:TPU:6, one launch (start us, length us, event | category | flops | bytes accessed | tf_op | source)
XLA Modules:
  0.0 440.7 jit_solution(7493433449119299911)
XLA Ops:
  7.2 0.7 all-gather.2.cloned.1.call-update
  8.0 1.2 dynamic_slice.35
  9.2 1.2 dynamic_slice.34
  10.4 0.9 copy.28
  11.5 0.9 fusion.121
  12.6 0.6 iota_compare_fusion.1
  13.4 1.1 fusion.122
  14.9 107.0 %all-gather.2.cloned.1.call-done = bf16[2,8192,256]{2,1,0:T(8,128)(2,1)} async-done(((bf16[2,512,256]{2,1,0:T(8,128)(2,1)}), bf16[2,8192,256]{2,1,0:T(8,128)(2,1)}) %all-gather.2.cloned.1.call-update) | async-done | bytes 8388624 | tf_op jit(solution)/shard_map/all_gather | solution.py:85
  121.9 12.5 %reshape.277 = bf16[2,16,512,2,128]{4,3,2,1,0:T(2,128)(2,1)} reshape(bf16[2,8192,256]{2,1,0:T(8,128)(2,1)} %all-gather.2.cloned.1.call-done) | data formatting | bytes 16777216 | tf_op jit(solution)/shard_map/reshape | solution.py:87
  134.4 8.8 %copy.30 = bf16[2,16,512,2,128]{4,2,3,1,0:T(8,128)(2,1)} copy(bf16[2,16,512,2,128]{4,3,2,1,0:T(2,128)(2,1)} %reshape.277) | data formatting | bytes 16777216
  143.2 79.0 %while.20 = (s32[]{:T(128)}, f32[1,128,2,128]{1,3,2,0:T(8,128)S(1)}, f32[1,128,2]{1,2,0:T(2,128)S(1)}, f32[1,128,2]{1,2,0:T(2,128)S(1)}, s32[16]{0:T(128)S(1)}, ...) while((s32[]{:T(128)}, ...), condition=%wide.region_7.8_spmd.clone, body=%wide.region_2.7_spmd.clone.sunk | while | flops 68782248 | bytes 2980505 | solution.py:109
  143.2 0.6 dynamic_slice.54
  147.0 0.6 dynamic_slice.54
  150.7 4.7 %conditional.3 = ((f32[1,128,2,128]{1,3,2,0:T(8,128)S(1)}, f32[1,128,2]{1,2,0:T(2,128)S(1)}, f32[1,128,2]{1,2,0:T(2,128)S(1)})) conditional(s32[]{:T(128)} %bitcast.111, (f32[1,128,2,128]{1,3,2,0:T(8,128)S(1)}, f32[1,128,2]{1,2,0:T(2,128)S(1)}, f32[1,128,2]{1,2,0:T(2,128)S(1)}) %tuple.96, (pred[1]{0:T(512)(128)(4,1)}, s32[]{:T(128)}, ...), branch_computations={%region_3.3_spmd, %region_4.6_spmd.clone} | conditional | flops 68782224 | bytes 2977504 | solution.py:107
  152.8 1.2 fusion.120
  154.1 1.3 fusion.10
  155.4 0.6 dynamic_slice.54
  159.2 0.6 dynamic_slice.54
  162.9 0.6 dynamic_slice.54
  166.7 0.6 dynamic_slice.54
  170.5 0.6 dynamic_slice.54
  174.2 4.7 %conditional.3 = ((f32[1,128,2,128]{1,3,2,0:T(8,128)S(1)}, f32[1,128,2]{1,2,0:T(2,128)S(1)}, f32[1,128,2]{1,2,0:T(2,128)S(1)})) conditional(s32[]{:T(128)} %bitcast.111, (f32[1,128,2,128]{1,3,2,0:T(8,128)S(1)}, f32[1,128,2]{1,2,0:T(2,128)S(1)}, f32[1,128,2]{1,2,0:T(2,128)S(1)}) %tuple.96, (pred[1]{0:T(512)(128)(4,1)}, s32[]{:T(128)}, ...), branch_computations={%region_3.3_spmd, %region_4.6_spmd.clone} | conditional | flops 68782224 | bytes 2977504 | solution.py:107
  176.3 1.2 fusion.120
  177.7 1.3 fusion.10
  178.9 0.6 dynamic_slice.54
  182.7 0.6 dynamic_slice.54
  186.5 0.6 dynamic_slice.54
  190.2 4.7 %conditional.3 = ((f32[1,128,2,128]{1,3,2,0:T(8,128)S(1)}, f32[1,128,2]{1,2,0:T(2,128)S(1)}, f32[1,128,2]{1,2,0:T(2,128)S(1)})) conditional(s32[]{:T(128)} %bitcast.111, (f32[1,128,2,128]{1,3,2,0:T(8,128)S(1)}, f32[1,128,2]{1,2,0:T(2,128)S(1)}, f32[1,128,2]{1,2,0:T(2,128)S(1)}) %tuple.96, (pred[1]{0:T(512)(128)(4,1)}, s32[]{:T(128)}, ...), branch_computations={%region_3.3_spmd, %region_4.6_spmd.clone} | conditional | flops 68782224 | bytes 2977504 | solution.py:107
  192.3 1.2 fusion.120
  193.6 1.3 fusion.10
  194.9 0.6 dynamic_slice.54
  198.7 0.6 dynamic_slice.54
  202.4 0.6 dynamic_slice.54
  206.2 0.6 dynamic_slice.54
  210.0 0.6 dynamic_slice.54
  213.7 0.6 dynamic_slice.54
  217.5 4.7 %conditional.3 = ((f32[1,128,2,128]{1,3,2,0:T(8,128)S(1)}, f32[1,128,2]{1,2,0:T(2,128)S(1)}, f32[1,128,2]{1,2,0:T(2,128)S(1)})) conditional(s32[]{:T(128)} %bitcast.111, (f32[1,128,2,128]{1,3,2,0:T(8,128)S(1)}, f32[1,128,2]{1,2,0:T(2,128)S(1)}, f32[1,128,2]{1,2,0:T(2,128)S(1)}) %tuple.96, (pred[1]{0:T(512)(128)(4,1)}, s32[]{:T(128)}, ...), branch_computations={%region_3.3_spmd, %region_4.6_spmd.clone} | conditional | flops 68782224 | bytes 2977504 | solution.py:107
  219.5 1.2 fusion.120
  220.9 1.3 fusion.10
  223.1 1.2 convert_element_type.80
  224.3 132.2 %all-reduce.2.cloned.1.call-done = bf16[128,4096]{1,0:T(8,128)(2,1)} async-done(((bf16[128,4096]{1,0:T(8,128)(2,1)}), bf16[128,4096]{1,0:T(8,128)(2,1)}) %all-reduce.2.cloned.1.call-update) | async-done | bytes 1048592 | tf_op jit(solution)/shard_map/psum | solution.py:122
  356.5 1.5 convert_reduce_fusion
  358.1 1.7 multiply_reduce_fusion
  359.8 6.4 %convolution_convert_fusion = bf16[128,4096]{1,0:T(8,128)(2,1)} fusion(bf16[512,4096]{1,0:T(8,128)(2,1)} %param.22, bf16[4096,512]{1,0:T(8,128)(2,1)} %param.21, bf16[128,4096]{1,0:T(8,128)(2,1)S(1)} %copy-done.1, f32[4096]{0:T(1024)S(1)} %copy-done.3, f32[128]{0:T(128)S(1)} %add_rsqrt_fusion, f32[128]{0:T(128)S(1)} %broadcast_multiply_fusion), kind=kOutput, calls=%fused_computation.40 | convolution fusion | flops 1081147392 | bytes 10503168 | tf_op jit(solution)/shard_map/dot_general | solution.py:130
  366.2 0.7 copy.32
  367.0 1.6 convert_element_type.81
  368.5 63.9 %reduce-scatter.2.cloned.1.call-done = bf16[128,256]{1,0:T(8,128)(2,1)} async-done(((bf16[128,4096]{1,0:T(8,128)(2,1)}), bf16[128,256]{1,0:T(8,128)(2,1)}) %reduce-scatter.2.cloned.1.call-update) | async-done | bytes 65552 | tf_op jit(solution)/shard_map/reduce_scatter | solution.py:131
  432.5 1.7 select_convert_fusion
  (122 shorter events, 3.5 us)
Async XLA Ops:
  7.2 215.1 %copy-start = (bf16[256,4096]{1,0:T(8,128)(2,1)S(1)}, bf16[256,4096]{1,0:T(8,128)(2,1)}, u32[]{:S(2)}) copy-start(bf16[256,4096]{1,0:T(8,128)(2,1)} %param.20) | copy-start | bytes 6291460
  7.2 114.7 %all-gather.2.cloned.1.call-start = ((), (), s32[]{:S(2)}) async-start(), calls=%async_computation.1 | async-start | bytes 8912896 | tf_op jit(solution)/shard_map/all_gather | solution.py:85
  7.9 348.6 %all-reduce.2.cloned.1.call-start = ((), (), s32[]{:S(2)}) async-start(), calls=%async_computation.2 | async-start | bytes 2097152 | tf_op jit(solution)/shard_map/psum | solution.py:122
  134.4 8.8 %copy-start.4 = (s32[16]{0:T(128)S(1)}, s32[16]{0:T(128)}, u32[]{:S(2)}) copy-start(s32[16]{0:T(128)} %param.25) | copy-start | bytes 196
  222.2 0.8 copy-start.2
  224.3 135.5 %copy-start.3 = (f32[4096]{0:T(1024)S(1)}, f32[4096]{0:T(1024)}, u32[]{:S(2)}) copy-start(f32[4096]{0:T(1024)} %param.19) | copy-start | bytes 49156
  224.3 208.2 %reduce-scatter.2.cloned.1.call-start = ((), (), s32[]{:S(2)}) async-start(), calls=%async_computation.3 | async-start | bytes 1114112 | tf_op jit(solution)/shard_map/reduce_scatter | solution.py:131
  356.5 3.2 copy-start.1
Sparse Core Ops, SparseCore 0:
  10.4 111.4 all-gather.1
  224.4 132.0 all-reduce.1
  366.3 66.0 reduce-scatter.1
where the time goes:
time: 442 us; the launch traced here: 441 us
  waiting for transfers between devices  304 us (69%)
  loops' own time  58.2 us (13%)
  local copies, waits for them, and re-layouts  36.9 us (8%)
  matrix products  18.1 us (4%)
  between operations  13.9 us (3%)
  other arithmetic  9.68 us (2%)
    psum x1, waiting for transfers between devices, shards(): lax.psum(head_term.astype(jnp.bfloat16), 'mp').astype(jnp.float32)  132 us
    all_gather x1, waiting for transfers between devices, shards(): shard_piece = lax.all_gather(prefix_kv, 'req', axis=1, tiled=True)  107 us
    reduce_scatter x1, waiting for transfers between devices, shards(): lax.psum_scatter(projected.astype(jnp.bfloat16), 'mp', scatter_dimension=...  63.9 us
    another operation x1, loops' own time, shards(): result = lax.fori_loop(0, block_total, fold_step, own_part)  50.1 us
    reshape x1, local copies, waits for them, and re-layouts, shards(): blocks_here = shard_piece.reshape(2, block_total, KB, head_count, DH)  12.5 us
    unnamed x17, local copies, waits for them, and re-layouts  11.3 us
    dynamic_slice x16, local copies, waits for them, and re-layouts, fold_step(): logical = prefix_owner[block_index]  9.59 us
  transfers between devices with their start and end apart: 3, of which 3 were waited for; matrix products, arithmetic and copies ran while one was open for 2% of the time, Pallas kernels for 0%

commit v1 on v0

--- a/solution.py
+++ b/solution.py
@@ -9,6 +9,9 @@
 S_MAX = 128
 P_SIZE = 2048
 very_negative = -1e30
+register_rows_by_axis = lambda frame_in, axis_tag: jnp.sum(
+    lax.all_gather(frame_in, axis_name=axis_tag), axis=0
+)
 
 
 def block_partial(query_rows, key_rows, value_rows, query_pos, key_pos, allowed, slopes, shared):
@@ -119,7 +122,7 @@
         jnp.float32
     )
     head_term = lax.dynamic_update_slice_in_dim(head_term, own_columns, col_start, 1)
-    mixed_rows = lax.psum(head_term.astype(jnp.bfloat16), "mp").astype(jnp.float32)
+    mixed_rows = register_rows_by_axis(head_term.astype(jnp.bfloat16), "mp").astype(jnp.float32)
     row_mean = jnp.mean(mixed_rows, axis=1, keepdims=True)
     centered = mixed_rows - row_mean
     variance = jnp.mean(centered * centered, axis=1, keepdims=True)

time: 442 us -> 418 us (0.946)
  waiting for transfers between devices: 304 us -> 273 us
  other arithmetic: 9.68 us -> 16 us
    psum x1 -> x0, waiting for transfers between devices: 132 us -> none  [shards(): lax.psum(head_term.astype(jnp.bfloat16), 'mp').astype(jnp.float32)]
    all_gather x0 -> x1, waiting for transfers between devices: none -> 101 us  [lax.all_gather(frame_in, axis_name=axis_tag)]
    reduce_sum x0 -> x1, other arithmetic: none -> 8.93 us  [jnp.sum(lax.all_gather(frame_in, axis_name=axis_tag), axis=0)]
    unnamed x17 -> x15, local copies, waits for them, and re-layouts: 11.3 us -> 11.4 us
where the time goes in v1:
time: 418 us; the launch traced here: 416 us
  waiting for transfers between devices  273 us (65%)
  loops' own time  58.2 us (14%)
  local copies, waits for them, and re-layouts  36.9 us (9%)
  matrix products  18.1 us (4%)
  other arithmetic  16 us (4%)
  between operations  13.9 us (3%)
    all_gather x1, waiting for transfers between devices, shards(): shard_piece = lax.all_gather(prefix_kv, 'req', axis=1, tiled=True)  107 us
    all_gather x1, waiting for transfers between devices, lax.all_gather(frame_in, axis_name=axis_tag)  101 us
    reduce_scatter x1, waiting for transfers between devices, shards(): lax.psum_scatter(projected.astype(jnp.bfloat16), 'mp', scatter_dimension=...  63.6 us
    another operation x1, loops' own time, shards(): result = lax.fori_loop(0, block_total, fold_step, own_part)  50.1 us
    reshape x1, local copies, waits for them, and re-layouts, shards(): blocks_here = shard_piece.reshape(2, block_total, KB, head_count, DH)  12.5 us
    unnamed x15, local copies, waits for them, and re-layouts  11.4 us
    dynamic_slice x16, local copies, waits for them, and re-layouts, fold_step(): logical = prefix_owner[block_index]  9.59 us
    reduce_sum x1, other arithmetic, jnp.sum(lax.all_gather(frame_in, axis_name=axis_tag), axis=0)  8.93 us
  transfers between devices with their start and end apart: 3, of which 3 were waited for; matrix products, arithmetic and copies ran while one was open for 2% of the time, Pallas kernels for 0%

profile of v1, /device:TPU:6, one launch (start us, length us, event | category | flops | bytes accessed | tf_op | source)
XLA Modules:
  0.0 415.9 jit_solution(7991976849089987524)
XLA Ops:
  7.2 0.7 all-gather.4.cloned.1.call-update
  8.0 1.2 dynamic_slice.35
  9.2 1.2 dynamic_slice.34
  10.4 0.9 copy.28
  11.5 0.9 fusion.121
  12.6 0.6 iota_compare_fusion.1
  13.4 1.1 fusion.122
  14.9 107.0 %all-gather.4.cloned.1.call-done = bf16[2,8192,256]{2,1,0:T(8,128)(2,1)} async-done(((bf16[2,512,256]{2,1,0:T(8,128)(2,1)}), bf16[2,8192,256]{2,1,0:T(8,128)(2,1)}) %all-gather.4.cloned.1.call-update) | async-done | bytes 8388624 | tf_op jit(solution)/shard_map/all_gather | solution.py:88
  121.9 12.5 %reshape.278 = bf16[2,16,512,2,128]{4,3,2,1,0:T(2,128)(2,1)} reshape(bf16[2,8192,256]{2,1,0:T(8,128)(2,1)} %all-gather.4.cloned.1.call-done) | data formatting | bytes 16777216 | tf_op jit(solution)/shard_map/reshape | solution.py:90
  134.4 8.8 %copy.30 = bf16[2,16,512,2,128]{4,2,3,1,0:T(8,128)(2,1)} copy(bf16[2,16,512,2,128]{4,3,2,1,0:T(2,128)(2,1)} %reshape.278) | data formatting | bytes 16777216
  143.2 79.0 %while.20 = (s32[]{:T(128)}, f32[1,128,2,128]{1,3,2,0:T(8,128)S(1)}, f32[1,128,2]{1,2,0:T(2,128)S(1)}, f32[1,128,2]{1,2,0:T(2,128)S(1)}, s32[16]{0:T(128)S(1)}, ...) while((s32[]{:T(128)}, ...), condition=%wide.region_7.8_spmd.clone, body=%wide.region_2.7_spmd.clone.sunk | while | flops 68782248 | bytes 2980505 | solution.py:112
  143.2 0.6 dynamic_slice.54
  147.0 0.6 dynamic_slice.54
  150.7 4.7 %conditional.3 = ((f32[1,128,2,128]{1,3,2,0:T(8,128)S(1)}, f32[1,128,2]{1,2,0:T(2,128)S(1)}, f32[1,128,2]{1,2,0:T(2,128)S(1)})) conditional(s32[]{:T(128)} %bitcast.112, (f32[1,128,2,128]{1,3,2,0:T(8,128)S(1)}, f32[1,128,2]{1,2,0:T(2,128)S(1)}, f32[1,128,2]{1,2,0:T(2,128)S(1)}) %tuple.96, (pred[1]{0:T(512)(128)(4,1)}, s32[]{:T(128)}, ...), branch_computations={%region_3.3_spmd, %region_4.6_spmd.clone} | conditional | flops 68782224 | bytes 2977504 | solution.py:110
  152.8 1.2 fusion.120
  154.1 1.3 fusion.10
  155.4 0.6 dynamic_slice.54
  159.2 0.6 dynamic_slice.54
  162.9 0.6 dynamic_slice.54
  166.7 0.6 dynamic_slice.54
  170.5 0.6 dynamic_slice.54
  174.2 4.7 %conditional.3 = ((f32[1,128,2,128]{1,3,2,0:T(8,128)S(1)}, f32[1,128,2]{1,2,0:T(2,128)S(1)}, f32[1,128,2]{1,2,0:T(2,128)S(1)})) conditional(s32[]{:T(128)} %bitcast.112, (f32[1,128,2,128]{1,3,2,0:T(8,128)S(1)}, f32[1,128,2]{1,2,0:T(2,128)S(1)}, f32[1,128,2]{1,2,0:T(2,128)S(1)}) %tuple.96, (pred[1]{0:T(512)(128)(4,1)}, s32[]{:T(128)}, ...), branch_computations={%region_3.3_spmd, %region_4.6_spmd.clone} | conditional | flops 68782224 | bytes 2977504 | solution.py:110
  176.3 1.2 fusion.120
  177.7 1.3 fusion.10
  178.9 0.6 dynamic_slice.54
  182.7 0.6 dynamic_slice.54
  186.5 0.6 dynamic_slice.54
  190.2 4.7 %conditional.3 = ((f32[1,128,2,128]{1,3,2,0:T(8,128)S(1)}, f32[1,128,2]{1,2,0:T(2,128)S(1)}, f32[1,128,2]{1,2,0:T(2,128)S(1)})) conditional(s32[]{:T(128)} %bitcast.112, (f32[1,128,2,128]{1,3,2,0:T(8,128)S(1)}, f32[1,128,2]{1,2,0:T(2,128)S(1)}, f32[1,128,2]{1,2,0:T(2,128)S(1)}) %tuple.96, (pred[1]{0:T(512)(128)(4,1)}, s32[]{:T(128)}, ...), branch_computations={%region_3.3_spmd, %region_4.6_spmd.clone} | conditional | flops 68782224 | bytes 2977504 | solution.py:110
  192.3 1.2 fusion.120
  193.6 1.3 fusion.10
  194.9 0.6 dynamic_slice.54
  198.7 0.6 dynamic_slice.54
  202.4 0.6 dynamic_slice.54
  206.2 0.6 dynamic_slice.54
  210.0 0.6 dynamic_slice.54
  213.7 0.6 dynamic_slice.54
  217.5 4.7 %conditional.3 = ((f32[1,128,2,128]{1,3,2,0:T(8,128)S(1)}, f32[1,128,2]{1,2,0:T(2,128)S(1)}, f32[1,128,2]{1,2,0:T(2,128)S(1)})) conditional(s32[]{:T(128)} %bitcast.112, (f32[1,128,2,128]{1,3,2,0:T(8,128)S(1)}, f32[1,128,2]{1,2,0:T(2,128)S(1)}, f32[1,128,2]{1,2,0:T(2,128)S(1)}) %tuple.96, (pred[1]{0:T(512)(128)(4,1)}, s32[]{:T(128)}, ...), branch_computations={%region_3.3_spmd, %region_4.6_spmd.clone} | conditional | flops 68782224 | bytes 2977504 | solution.py:110
  219.5 1.2 fusion.120
  220.9 1.3 fusion.10
  222.2 0.5 fusion.123
  223.1 1.1 convert_element_type.82
  224.3 101.4 %all-gather.6.cloned.1.call-done = bf16[2048,4096]{1,0:T(8,128)(2,1)} async-done(((bf16[128,4096]{1,0:T(8,128)(2,1)}), bf16[2048,4096]{1,0:T(8,128)(2,1)}) %all-gather.6.cloned.1.call-update) | async-done | bytes 16777232 | tf_op jit(solution)/shard_map/all_gather | solution.py:13
  325.7 8.9 %reduce_sum.54 = bf16[128,4096]{1,0:T(8,128)(2,1)S(1)} reduce(bf16[16,128,4096]{2,1,0:T(8,128)(2,1)} %bitcast.113, bf16[]{:T(256)} %constant.205.clone.1), dimensions={0}, to_apply=%region_8.9 | reduce | flops 7864320 | bytes 17825794 | tf_op jit(solution)/shard_map/reduce_sum | solution.py:12
  335.3 6.4 %convolution_convert_fusion = bf16[128,4096]{1,0:T(8,128)(2,1)} fusion(bf16[512,4096]{1,0:T(8,128)(2,1)} %param.22, bf16[4096,512]{1,0:T(8,128)(2,1)} %param.21, bf16[128,4096]{1,0:T(8,128)(2,1)S(1)} %reduce_sum.54, f32[4096]{0:T(1024)S(1)} %copy-done.2, f32[128]{0:T(128)S(1)} %add_rsqrt_fusion, f32[128]{0:T(128)S(1)} %broadcast_multiply_fusion), kind=kOutput, calls=%fused_computation.40 | convolution fusion | flops 1081147392 | bytes 10503168 | tf_op jit(solution)/shard_map/dot_general | solution.py:133
  341.8 0.7 copy.32
  342.5 1.6 convert_element_type.83
  344.1 63.6 %reduce-scatter.2.cloned.1.call-done = bf16[128,256]{1,0:T(8,128)(2,1)} async-done(((bf16[128,4096]{1,0:T(8,128)(2,1)}), bf16[128,256]{1,0:T(8,128)(2,1)}) %reduce-scatter.2.cloned.1.call-update) | async-done | bytes 65552 | tf_op jit(solution)/shard_map/reduce_scatter | solution.py:134
  407.7 1.7 select_convert_fusion
  (121 shorter events, 3.7 us)
Async XLA Ops:
  7.2 215.1 %copy-start = (bf16[256,4096]{1,0:T(8,128)(2,1)S(1)}, bf16[256,4096]{1,0:T(8,128)(2,1)}, u32[]{:S(2)}) copy-start(bf16[256,4096]{1,0:T(8,128)(2,1)} %param.20) | copy-start | bytes 6291460
  7.2 114.7 %all-gather.4.cloned.1.call-start = ((), (), s32[]{:S(2)}) async-start(), calls=%async_computation.1 | async-start | bytes 8912896 | tf_op jit(solution)/shard_map/all_gather | solution.py:88
  7.9 317.8 %all-gather.6.cloned.1.call-start = ((), (), s32[]{:S(2)}) async-start(), calls=%async_computation.3 | async-start | bytes 17825792 | tf_op jit(solution)/shard_map/all_gather | solution.py:13
  134.4 8.8 %copy-start.3 = (s32[16]{0:T(128)S(1)}, s32[16]{0:T(128)}, u32[]{:S(2)}) copy-start(s32[16]{0:T(128)} %param.25) | copy-start | bytes 196
  222.2 0.8 copy-start.1
  224.3 183.5 %reduce-scatter.2.cloned.1.call-start = ((), (), s32[]{:S(2)}) async-start(), calls=%async_computation.2 | async-start | bytes 1114112 | tf_op jit(solution)/shard_map/reduce_scatter | solution.py:134
  334.6 0.7 copy-start.2
Sparse Core Ops, SparseCore 0:
  10.4 111.4 all-gather.3
  224.4 101.2 all-gather.5
  341.9 65.7 reduce-scatter.1
